TPU v7x, 32 devices: a whole 2x2x4 slice. The times are simulated.
32 devices in a mesh: grp: 4 (over z), tok: 8 (over y, x, core).
Axes of the slice: x: 2, y: 2, z: 4, core: 2. Of those that a mesh axis runs over, the one named last changes fastest.
Arguments:
- tokens: bfloat16 [8192, 2048], P(('grp', 'tok')), may hold values from -6 to 6
- cotangent: bfloat16 [8192, 2048], P(('grp', 'tok')), may hold values from -6 to 6
- norm_gain: bfloat16 [2048], P(('grp', 'tok')), may hold values from 0.099609375 to 1.8984375
- norm_bias: bfloat16 [2048], P(('grp', 'tok')), may hold values from -3 to 3
- joint_weight: bfloat16 [2048, 6144], P(('grp', 'tok')), may hold values from -0.125 to 0.125
- out_weight: bfloat16 [2048, 2048], P(('grp', 'tok')), may hold values from -2 to 2
- gate_weight: bfloat16 [2048, 5632], P(('grp', 'tok')), may hold values from -0.125 to 0.125
- up_weight: bfloat16 [2048, 5632], P(('grp', 'tok')), may hold values from -0.125 to 0.125
- down_weight: bfloat16 [5632, 2048], P(('grp', 'tok')), may hold values from -0.078125 to 0.078125
- block_table: int32 [4, 16], P('grp'), may hold values from 0 to 15, each once within a row
Outputs:
- result: bfloat16 [8192, 2048], P(('grp', 'tok'))
- input_grad: bfloat16 [8192, 2048], P(('grp', 'tok'))
- gain_grad: float32 [2048], P(('grp', 'tok'))
- bias_grad: float32 [2048], P(('grp', 'tok'))
- joint_grad: float32 [2048, 6144], P(('grp', 'tok'))
- out_grad: float32 [2048, 2048], P(('grp', 'tok'))
- gate_grad: float32 [2048, 5632], P(('grp', 'tok'))
- up_grad: float32 [2048, 5632], P(('grp', 'tok'))
- down_grad: float32 [5632, 2048], P(('grp', 'tok'))
Inputs may be any that keep to these rules, and one draw needn't show every extreme that they name: Each row of block_table is a permutation; value v in a slot of grp index r places there block v % 16 of group v // 16 of that index: a prompt block if v % 16 < 8, else one continuation.
All inputs are finite; a program needn't handle non-finite values.
Results may differ from a plain program's by a relative error of at most 0.012.
Values may be sent and summed in bfloat16 or wider, within the bound.
No kernel may reach another device: no remote copies, remote signals or barrier semaphores. Data moves between devices by JAX's collectives and lax.ppermute only.
A program may use at most 640 MiB of HBM per device.

v0:
```python
import jax
import jax.numpy as jnp
from jax import lax
from jax.sharding import PartitionSpec as P

HD = 64
ROT = 16
FF = 5632
BT = 128
PB = 8
BLK_GROUP = 16
PROMPT = 1024
KEY_BLK = 256
eps = 1e-05
neg_big = -1e30


def spread_blocks(values):
    return jnp.repeat(values, BT, axis=-1)


def token_tables(slots):
    part_of = slots % BLK_GROUP
    group_of = slots // BLK_GROUP
    is_prompt = part_of < PB
    begins = jnp.where(is_prompt, part_of * BT, PROMPT)
    offsets = jnp.arange(BT, dtype=jnp.int32)
    position = (begins[:, None] + offsets[None, :]).reshape(-1)
    return (position, spread_blocks(group_of), spread_blocks(part_of), spread_blocks(is_prompt))


def permitted(query_info, key_info):
    q_pos, q_grp, q_part = query_info
    k_pos, k_grp, k_part, k_prompt = key_info
    same = q_grp[:, None] == k_grp[None, :]
    causal = k_pos[None, :] <= q_pos[:, None]
    either = k_prompt[None, :] | (k_part[None, :] == q_part[:, None])
    return same & causal & either


def frequencies():
    return 10000.0 ** (-jnp.arange(0, ROT, 2, dtype=jnp.float32) / ROT)


def turn(values, cosine, sine):
    half = ROT // 2
    first = values[..., :half]
    second = values[..., half:ROT]
    return jnp.concatenate(
        [first * cosine - second * sine, second * cosine + first * sine, values[..., ROT:]], axis=-1
    )


def inner(left, right):
    return lax.dot_general(
        left, right, (((0,), (0,)), ((), ())), preferred_element_type=jnp.float32
    )


def body(
    tokens,
    cotangent,
    norm_gain,
    norm_bias,
    joint_weight,
    out_weight,
    gate_weight,
    up_weight,
    down_weight,
    block_table,
):
    rows = tokens.shape[0]
    width = tokens.shape[1]
    heads = width // HD
    scale = HD ** (-0.5)
    gathered = (
        lax.all_gather(norm_gain, ("grp", "tok"), axis=0, tiled=True),
        lax.all_gather(norm_bias, ("grp", "tok"), axis=0, tiled=True),
        lax.all_gather(joint_weight, ("grp", "tok"), axis=0, tiled=True),
        lax.all_gather(out_weight, ("grp", "tok"), axis=0, tiled=True),
        lax.all_gather(gate_weight, ("grp", "tok"), axis=0, tiled=True),
        lax.all_gather(up_weight, ("grp", "tok"), axis=0, tiled=True),
        lax.all_gather(down_weight, ("grp", "tok"), axis=0, tiled=True),
    )
    gain_full = gathered[0].astype(jnp.float32)
    bias_full = gathered[1].astype(jnp.float32)
    joint_full, out_full, gate_full, up_full, down_full = gathered[2:]
    position, group_tok, part_tok, prompt_tok = token_tables(block_table[0])
    first_row = lax.axis_index("tok") * rows

    def mine(values):
        return lax.dynamic_slice_in_dim(values, first_row, rows)

    query_info = (mine(position), mine(group_tok), mine(part_tok))
    inputs = tokens.astype(jnp.float32)
    mean = jnp.mean(inputs, axis=-1, keepdims=True)
    centred = inputs - mean
    inv_std = lax.rsqrt(jnp.mean(centred * centred, axis=-1, keepdims=True) + eps)
    normed = centred * inv_std
    hidden_in = (normed * gain_full + bias_full).astype(jnp.bfloat16)
    joint = jnp.dot(hidden_in, joint_full, preferred_element_type=jnp.float32)
    angles = query_info[0].astype(jnp.float32)[:, None] * frequencies()[None, :]
    cosine = jnp.cos(angles)[:, None, :]
    sine = jnp.sin(angles)[:, None, :]
    query = turn(joint[:, :width].reshape(rows, heads, HD), cosine, sine).astype(jnp.bfloat16)
    key_mine = (
        turn(joint[:, width : 2 * width].reshape(rows, heads, HD), cosine, sine)
        .astype(jnp.bfloat16)
        .reshape(rows, width)
    )
    value_mine = joint[:, 2 * width :].astype(jnp.bfloat16)
    key_all, value_all = (
        lax.all_gather(key_mine, "tok", axis=0, tiled=True),
        lax.all_gather(value_mine, "tok", axis=0, tiled=True),
    )
    blocks = key_all.shape[0] // KEY_BLK
    key_blocks = key_all.reshape(blocks, KEY_BLK, heads, HD)
    value_blocks = value_all.reshape(blocks, KEY_BLK, heads, HD)
    key_info = (
        position.reshape(blocks, KEY_BLK),
        group_tok.reshape(blocks, KEY_BLK),
        part_tok.reshape(blocks, KEY_BLK),
        prompt_tok.reshape(blocks, KEY_BLK),
    )

    def scores(key_block):
        return (
            jnp.einsum("qhd,khd->hqk", query, key_block, preferred_element_type=jnp.float32) * scale
        )

    def lse_step(carry, item):
        key_block = item[0]
        allowed = permitted(query_info, item[1:])
        masked = jnp.where(allowed[None], scores(key_block), neg_big)
        top = jnp.maximum(carry[0], jnp.max(masked, axis=2))
        terms = jnp.where(allowed[None], jnp.exp(masked - top[:, :, None]), 0.0)
        return ((top, carry[1] * jnp.exp(carry[0] - top) + jnp.sum(terms, axis=2)), None)

    start = (jnp.full((heads, rows), neg_big, jnp.float32), jnp.zeros((heads, rows), jnp.float32))
    (top_all, total_all), _ = lax.scan(lse_step, start, (key_blocks,) + key_info)
    log_total = top_all + jnp.log(total_all)

    def probabilities(raw, allowed):
        masked = jnp.where(allowed[None], raw, neg_big)
        return jnp.where(allowed[None], jnp.exp(masked - log_total[:, :, None]), 0.0)

    def out_step(carry, item):
        key_block, value_block = (item[0], item[1])
        allowed = permitted(query_info, item[2:])
        weights = probabilities(scores(key_block), allowed).astype(jnp.bfloat16)
        return (
            carry
            + jnp.einsum("hqk,khd->qhd", weights, value_block, preferred_element_type=jnp.float32),
            None,
        )

    attended, _ = lax.scan(
        out_step, jnp.zeros((rows, heads, HD), jnp.float32), (key_blocks, value_blocks) + key_info
    )
    attended = attended.reshape(rows, width)
    attended_low = attended.astype(jnp.bfloat16)
    branch_attn = jnp.dot(attended_low, out_full, preferred_element_type=jnp.float32)
    gate = jnp.dot(hidden_in, gate_full, preferred_element_type=jnp.float32)
    up = jnp.dot(hidden_in, up_full, preferred_element_type=jnp.float32)
    sigma = jax.nn.sigmoid(gate)
    swish = gate * sigma
    activated = (swish * up).astype(jnp.bfloat16)
    branch_ff = jnp.dot(activated, down_full, preferred_element_type=jnp.float32)
    result = (inputs + branch_attn + branch_ff).astype(jnp.bfloat16)
    again = (
        lax.all_gather(norm_gain, ("grp", "tok"), axis=0, tiled=True),
        lax.all_gather(joint_weight, ("grp", "tok"), axis=0, tiled=True),
        lax.all_gather(out_weight, ("grp", "tok"), axis=0, tiled=True),
        lax.all_gather(gate_weight, ("grp", "tok"), axis=0, tiled=True),
        lax.all_gather(up_weight, ("grp", "tok"), axis=0, tiled=True),
        lax.all_gather(down_weight, ("grp", "tok"), axis=0, tiled=True),
    )
    gain_back = again[0].astype(jnp.float32)
    joint_back, out_back, gate_back, up_back, down_back = again[1:]
    d_act = jnp.dot(cotangent, down_back.T, preferred_element_type=jnp.float32)
    d_gate = (d_act * up * sigma * (1.0 + gate * (1.0 - sigma))).astype(jnp.bfloat16)
    d_up = (d_act * swish).astype(jnp.bfloat16)
    d_attended = jnp.dot(cotangent, out_back.T, preferred_element_type=jnp.float32).astype(
        jnp.bfloat16
    )
    d_heads = d_attended.reshape(rows, heads, HD)
    delta = jnp.einsum(
        "qhd,qhd->hq", d_heads.astype(jnp.float32), attended.reshape(rows, heads, HD)
    )

    def back_step(carry, item):
        key_block, value_block = (item[0], item[1])
        allowed = permitted(query_info, item[2:])
        weights = probabilities(scores(key_block), allowed)
        d_value = jnp.einsum(
            "hqk,qhd->khd",
            weights.astype(jnp.bfloat16),
            d_heads,
            preferred_element_type=jnp.float32,
        )
        d_weights = jnp.einsum(
            "qhd,khd->hqk", d_heads, value_block, preferred_element_type=jnp.float32
        )
        d_scores = (weights * (d_weights - delta[:, :, None])).astype(jnp.bfloat16)
        d_query = (
            carry
            + jnp.einsum("hqk,khd->qhd", d_scores, key_block, preferred_element_type=jnp.float32)
            * scale
        )
        d_key = (
            jnp.einsum("hqk,qhd->khd", d_scores, query, preferred_element_type=jnp.float32) * scale
        )
        return (d_query, (d_key, d_value))

    d_query, (d_keys, d_values) = lax.scan(
        back_step, jnp.zeros((rows, heads, HD), jnp.float32), (key_blocks, value_blocks) + key_info
    )
    d_key_mine, d_value_mine = (
        lax.psum_scatter(
            d_keys.reshape(-1, width).astype(jnp.bfloat16), "tok", scatter_dimension=0, tiled=True
        ).astype(jnp.float32),
        lax.psum_scatter(
            d_values.reshape(-1, width).astype(jnp.bfloat16), "tok", scatter_dimension=0, tiled=True
        ).astype(jnp.float32),
    )
    d_query_turned = turn(d_query, cosine, -sine).reshape(rows, width)
    d_key_turned = turn(d_key_mine.reshape(rows, heads, HD), cosine, -sine).reshape(rows, width)
    d_joint = jnp.concatenate([d_query_turned, d_key_turned, d_value_mine], axis=1).astype(
        jnp.bfloat16
    )
    d_hidden = jnp.dot(d_joint, joint_back.T, preferred_element_type=jnp.float32)
    d_hidden = d_hidden + jnp.dot(d_gate, gate_back.T, preferred_element_type=jnp.float32)
    d_hidden = d_hidden + jnp.dot(d_up, up_back.T, preferred_element_type=jnp.float32)
    d_normed = d_hidden * gain_back
    d_inputs = inv_std * (
        d_normed
        - jnp.mean(d_normed, axis=-1, keepdims=True)
        - normed * jnp.mean(d_normed * normed, axis=-1, keepdims=True)
    )
    input_grad = (cotangent.astype(jnp.float32) + d_inputs).astype(jnp.bfloat16)
    down_term = inner(activated, cotangent)
    gain_term = jnp.sum(d_hidden * normed, axis=0)
    bias_term = jnp.sum(d_hidden, axis=0)
    joined = lax.psum_scatter(
        jnp.concatenate(
            [
                inner(hidden_in, d_joint),
                inner(attended_low, cotangent),
                inner(hidden_in, d_gate),
                inner(hidden_in, d_up),
            ],
            axis=1,
        ),
        ("grp", "tok"),
        scatter_dimension=0,
        tiled=True,
    )
    down_grad, gain_grad, bias_grad = (
        lax.psum_scatter(down_term, ("grp", "tok"), scatter_dimension=0, tiled=True),
        lax.psum_scatter(gain_term, ("grp", "tok"), scatter_dimension=0, tiled=True),
        lax.psum_scatter(bias_term, ("grp", "tok"), scatter_dimension=0, tiled=True),
    )
    joint_grad = joined[:, : 3 * width]
    out_grad = joined[:, 3 * width : 4 * width]
    gate_grad = joined[:, 4 * width : 4 * width + FF]
    up_grad = joined[:, 4 * width + FF :]
    return (
        result,
        input_grad,
        gain_grad,
        bias_grad,
        joint_grad,
        out_grad,
        gate_grad,
        up_grad,
        down_grad,
    )


def solution(mesh):
    placed = (
        P(("grp", "tok"), None),
        P(("grp", "tok"), None),
        P(("grp", "tok")),
        P(("grp", "tok")),
        P(("grp", "tok"), None),
        P(("grp", "tok"), None),
        P(("grp", "tok"), None),
        P(("grp", "tok"), None),
        P(("grp", "tok"), None),
        P("grp", None),
    )
    return jax.shard_map(
        body,
        mesh=mesh,
        in_specs=placed,
        out_specs=(
            P(("grp", "tok"), None),
            P(("grp", "tok"), None),
            P(("grp", "tok")),
            P(("grp", "tok")),
            P(("grp", "tok"), None),
            P(("grp", "tok"), None),
            P(("grp", "tok"), None),
            P(("grp", "tok"), None),
            P(("grp", "tok"), None),
        ),
        check_vma=False,
    )
```

profile of v0, /device:TPU:1, one launch (start us, length us, event | category | flops | bytes accessed | tf_op | source)
XLA Modules:
  0.0 3242.4 jit_solution(7060317920040438360)
XLA Ops:
  10.4 42.9 %all-reduce.5 = (bf16[2048]{0:T(1024)(128)(2,1)S(1)}, bf16[2048]{0:T(1024)(128)(2,1)S(1)}) all-reduce(bf16[2048]{0:T(1024)(128)(2,1)S(1)} %dynamic-update-slice.1, bf16[2048]{0:T(1024)(128)(2,1)S(1)} %dynamic-update-slice), channel_id=1, replica_groups=mesh['grp'=4,'tok'=8] {'grp','tok'}, use_global_device_ids=true, to_apply=%add.1 | all-reduce | flops 4096 | bytes 16384
  58.0 111.4 %all-gather.8.cloned.1.call-done = bf16[2048,6144]{1,0:T(8,128)(2,1)} async-done(((bf16[64,6144]{1,0:T(8,128)(2,1)}), bf16[2048,6144]{1,0:T(8,128)(2,1)}) %all-gather.8.cloned.1.call-update) | async-done | bytes 25165840 | tf_op jit(solution)/shard_map/all_gather | solution.py:79
  169.4 11.8 fusion.85
  200.2 47.7 %all-gather.14.cloned.1.call-done = bf16[2048,2048]{1,0:T(8,128)(2,1)} async-done(((bf16[64,2048]{1,0:T(8,128)(2,1)}), bf16[2048,2048]{1,0:T(8,128)(2,1)}) %all-gather.14.cloned.1.call-update) | async-done | bytes 8388624 | tf_op jit(solution)/shard_map/all_gather | solution.py:80
  248.0 6.7 convolution_convert_fusion
  259.2 45.9 %all-gather.12.cloned.1.call-done = bf16[2048,2048]{0,1:T(8,128)(2,1)} async-done(((bf16[256,2048]{0,1:T(8,128)(2,1)}), bf16[2048,2048]{0,1:T(8,128)(2,1)}) %all-gather.12.cloned.1.call-update) | async-done | bytes 8388624 | tf_op jit(solution)/shard_map/all_gather | solution.py:113
  305.0 10.6 copy.95
  315.6 9.0 copy.72
  324.6 41.3 %while.39 = (s32[]{:T(128)}, f32[32,256]{1,0:T(8,128)S(1)}, f32[32,256]{1,0:T(8,128)S(1)}, s32[256]{0:T(256)S(1)}, s32[8,256]{1,0:T(8,128)S(1)}, /*index=5*/s32[...) while((s32[]{:T(128)}, f32[32,256]{1,0:T(8,128)S(1)}, ...), condition=%wide.region_5.6_spmd.clone, body=%wide.region_2.5_spmd.clone.sunk | while | flops 285646848 | bytes 19510184 | solution.py:140
  365.9 24.5 reshape.533
  390.4 19.5 copy.71
  410.0 52.6 %while.40 = (s32[]{:T(128)}, f32[256,32,64]{0,2,1:T(8,128)}, bf16[8,256,32,64]{1,3,2,0:T(8,128)(2,1)}, s32[256]{0:T(256)S(1)}, s32[8,256]{1,0:T(8,128)S(1)}, /*i...) while((s32[]{:T(128)}, f32[256,32,64]{0,2,1:T(8,128)}, ...), condition=%wide.region_7.8_spmd.clone, body=%wide.region_6.7_spmd.clone.sunk | while | flops 548798464 | bytes 7518634 | solution.py:157
  410.4 5.7 bitcast_add_fusion.5
  416.4 6.4 bitcast_add_fusion.5
  423.0 6.4 bitcast_add_fusion.5
  429.6 6.4 bitcast_add_fusion.5
  436.3 6.4 bitcast_add_fusion.5
  442.9 6.4 bitcast_add_fusion.5
  449.6 6.4 bitcast_add_fusion.5
  456.2 6.4 bitcast_add_fusion.5
  464.8 121.7 %while.41 = (s32[]{:T(128)}, f32[256,32,64]{0,2,1:T(8,128)S(1)}, bf16[8,256,32,64]{1,3,2,0:T(8,128)(2,1)}, bf16[8,256,32,64]{1,3,2,0:T(8,128)(2,1)}, bf16[8,256,...) while((s32[]{:T(128)}, f32[256,32,64]{0,2,1:T(8,128)S(1)}, ...), condition=%wide.region_9.10_spmd.clone, body=%wide.region_8.9_spmd.clone.sunk | while | flops 1369833472 | bytes 57979896 | solution.py:215
  482.9 4.8 fusion.159
  498.4 4.7 fusion.159
  528.7 4.7 fusion.159
  543.8 4.7 fusion.159
  586.5 15.4 copy.76
  601.9 10.8 copy.96
  612.7 15.3 copy.77
  628.0 10.8 copy.97
  640.0 14.1 fusion.81
  654.7 13.2 fusion.83
  667.9 132.4 %all-gather.20.cloned.1.call-done = bf16[5632,2048]{1,0:T(8,128)(2,1)} async-done(((bf16[176,2048]{1,0:T(8,128)(2,1)}), bf16[5632,2048]{1,0:T(8,128)(2,1)}) %all-gather.20.cloned.1.call-update) | async-done | bytes 23068688 | tf_op jit(solution)/shard_map/all_gather | solution.py:83
  800.3 20.5 multiply_convert_fusion
  820.8 21.5 fusion.76
  842.3 20.8 fusion.78
  866.2 8.2 fusion.90
  877.7 70.4 %reduce-scatter.7.cloned.1.call-done = bf16[256,2048]{0,1:T(8,128)(2,1)} async-done(((bf16[2048,2048]{0,1:T(8,128)(2,1)}), bf16[256,2048]{0,1:T(8,128)(2,1)}) %reduce-scatter.7.cloned.1.call-update) | async-done | bytes 1048592 | tf_op jit(solution)/shard_map/reduce_scatter | solution.py:222
  948.0 19.0 fusion.69
  967.0 102.9 %pad_maximum_fusion = f32[2048,19456]{1,0:T(8,128)} fusion(f32[2048,5632]{1,0:T(8,128)} %fusion.76, f32[2048,5632]{1,0:T(8,128)} %fusion.78, f32[2048,2048]{1,0:T(8,128)} %fusion.90, f32[2048,6144]{1,0:T(8,128)} %fusion.69), kind=kLoop, calls=%fused_computation.67 | loop fusion | flops 119537664 | bytes 318767104 | tf_op jit(solution)/shard_map/concatenate | solution.py:245
  1071.1 20.6 fusion.91
  1093.3 5.9 convert_add_fusion
  1099.2 12.2 fusion.52
  1111.4 13.5 fusion.70
  1124.9 13.5 convolution_add_fusion.1
  1138.4 13.5 fusion.66
  1151.9 47.2 %all-reduce.4 = (f32[2048]{0:T(1024)S(1)}, f32[2048]{0:T(1024)S(1)}) all-reduce(f32[2048]{0:T(1024)S(1)} %get-tuple-element.483, f32[2048]{0:T(1024)S(1)} %get-tuple-element.486), channel_id=4, replica_groups=mesh['grp'=4,'tok'=8] {'grp','tok'}, use_global_device_ids=true, to_apply=%region_15.16.clone | all-reduce | flops 4096 | bytes 32768
  1203.7 1533.9 %reduce-scatter.9.cloned.1.call-done = f32[64,19456]{1,0:T(8,128)} async-done(((f32[2048,19456]{1,0:T(8,128)}), f32[64,19456]{1,0:T(8,128)}) %reduce-scatter.9.cloned.1.call-update) | async-done | bytes 4980752 | tf_op jit(solution)/shard_map/reduce_scatter | solution.py:244
  2745.7 489.9 %reduce-scatter.11.cloned.1.call-done = f32[176,2048]{1,0:T(8,128)} async-done(((f32[5632,2048]{1,0:T(8,128)}), f32[176,2048]{1,0:T(8,128)}) %reduce-scatter.11.cloned.1.call-update) | async-done | bytes 1441808 | tf_op jit(solution)/shard_map/reduce_scatter | solution.py:259
  (337 shorter events, 201.8 us)
Async XLA Ops:
  7.2 162.2 %copy-start = (bf16[256,2048]{1,0:T(8,128)(2,1)S(1)}, bf16[256,2048]{1,0:T(8,128)(2,1)}, u32[]{:S(2)}) copy-start(bf16[256,2048]{1,0:T(8,128)(2,1)} %param.16) | copy-start | bytes 3145732
  7.2 162.2 %all-gather.8.cloned.1.call-start = ((), (), s32[]{:S(2)}) async-start(), calls=%async_computation.4 | async-start | bytes 25952256 | tf_op jit(solution)/shard_map/all_gather | solution.py:79
  7.9 240.1 %all-gather.14.cloned.1.call-start = ((), (), s32[]{:S(2)}) async-start(), calls=%async_computation.7 | async-start | bytes 8650752 | tf_op jit(solution)/shard_map/all_gather | solution.py:80
  8.7 296.4 %all-gather.12.cloned.1.call-start = ((), (), s32[]{:S(2)}) async-start(), calls=%async_computation.6 | async-start | bytes 9437184 | tf_op jit(solution)/shard_map/all_gather | solution.py:113
  53.3 116.1 %copy-start.18 = (f32[2048]{0:T(1024)}, f32[2048]{0:T(1024)S(1)}, u32[]{:S(2)}) copy-start(f32[2048]{0:T(1024)S(1)} %convert_element_type.77) | copy-start | bytes 24580
  53.3 116.1 %copy-start.15 = (f32[2048]{0:T(1024)}, f32[2048]{0:T(1024)S(1)}, u32[]{:S(2)}) copy-start(f32[2048]{0:T(1024)S(1)} %convert_element_type.76) | copy-start | bytes 24580
  55.6 113.8 %copy-start.20 = (f32[256]{0:T(256)}, f32[256]{0:T(256)S(1)}, u32[]{:S(2)}) copy-start(f32[256]{0:T(256)S(1)} %broadcast_multiply_fusion.2) | copy-start | bytes 3076
  57.3 112.1 %copy-start.23 = (f32[256]{0:T(256)}, f32[256]{0:T(256)S(1)}, u32[]{:S(2)}) copy-start(f32[256]{0:T(256)S(1)} %add_rsqrt_fusion) | copy-start | bytes 3076
  58.0 132.8 %copy-start.26 = (f32[256,8]{0,1:T(8,128)}, f32[256,8]{0,1:T(8,128)S(1)}, u32[]{:S(2)}) copy-start(f32[256,8]{0,1:T(8,128)S(1)} %get-tuple-element.610) | copy-start | bytes 24580
  181.2 3.4 copy-start.8
  193.3 5.4 copy-start.29
  193.3 54.7 %copy-start.5 = (bf16[256,2048]{1,0:T(8,128)(2,1)S(1)}, bf16[256,2048]{1,0:T(8,128)(2,1)}, u32[]{:S(2)}) copy-start(bf16[256,2048]{1,0:T(8,128)(2,1)} %param.17) | copy-start | bytes 3145732
  193.3 172.6 %all-gather.10.cloned.1.call-start = ((), (), s32[]{:S(2)}) async-start(), calls=%async_computation.5 | async-start | bytes 9437184 | tf_op jit(solution)/shard_map/all_gather | solution.py:114
  196.2 442.7 %all-gather.18.cloned.1.call-start = ((), (), s32[]{:S(2)}) async-start(), calls=%async_computation.9 | async-start | bytes 23789568 | tf_op jit(solution)/shard_map/all_gather | solution.py:82
  196.8 457.9 %all-gather.16.cloned.1.call-start = ((), (), s32[]{:S(2)}) async-start(), calls=%async_computation.8 | async-start | bytes 23789568 | tf_op jit(solution)/shard_map/all_gather | solution.py:81
  197.3 603.0 %all-gather.20.cloned.1.call-start = ((), (), s32[]{:S(2)}) async-start(), calls=%async_computation.10 | async-start | bytes 23789568 | tf_op jit(solution)/shard_map/all_gather | solution.py:83
  198.1 676.4 %reduce-scatter.5.cloned.1.call-start = ((), (), s32[]{:S(2)}) async-start(), calls=%async_computation.11 | async-start | bytes 9437184 | tf_op jit(solution)/shard_map/reduce_scatter | solution.py:219
  465.1 2.6 copy-start.10
  480.3 2.6 copy-start.10
  495.5 2.9 copy-start.10
  511.0 2.6 copy-start.10
  526.0 2.6 copy-start.10
  541.2 2.6 copy-start.10
  556.2 2.6 copy-start.10
  571.4 2.6 copy-start.10
  612.7 335.4 %reduce-scatter.7.cloned.1.call-start = ((), (), s32[]{:S(2)}) async-start(), calls=%async_computation.12 | async-start | bytes 9437184 | tf_op jit(solution)/shard_map/reduce_scatter | solution.py:222
  638.8 1.2 copy-start.1
  638.8 1.2 copy-start.16
  638.8 1.2 copy-start.19
  638.8 1.2 copy-start.21
  638.8 1.2 copy-start.24
  638.8 2098.8 %reduce-scatter.9.cloned.1.call-start = ((), (), s32[]{:S(2)}) async-start(), calls=%async_computation.13 | async-start | bytes 164364288 | tf_op jit(solution)/shard_map/reduce_scatter | solution.py:244
  863.1 3.1 copy-start.6
  865.0 1.2 copy-start.3
  874.4 2.8 copy-start.27
  874.4 2.8 copy-start.28
  874.5 2.9 copy-start.14
  877.5 89.5 %copy-start.11 = (bf16[256,32,64]{0,2,1:T(8,128)(2,1)}, bf16[256,32,64]{0,2,1:T(8,128)(2,1)S(1)}, u32[]{:S(2)}) copy-start(bf16[256,32,64]{0,2,1:T(8,128)(2,1)S(1)} %pad_maximum_fusion.6) | copy-start | bytes 3145732
  877.6 89.4 %copy-start.13 = (bf16[256,32,64]{0,2,1:T(8,128)(2,1)}, bf16[256,32,64]{0,2,1:T(8,128)(2,1)S(1)}, u32[]{:S(2)}) copy-start(bf16[256,32,64]{0,2,1:T(8,128)(2,1)S(1)} %pad_maximum_fusion.7) | copy-start | bytes 3145732
  1069.9 1.2 copy-start.7
  1069.9 2165.7 %reduce-scatter.11.cloned.1.call-start = ((), (), s32[]{:S(2)}) async-start(), calls=%async_computation.14 | async-start | bytes 47579136 | tf_op jit(solution)/shard_map/reduce_scatter | solution.py:259
  1091.7 1.2 copy-start.2
  1091.7 1.5 copy-start.4
  1093.3 5.9 copy-start.9
  1099.2 12.2 copy-start.12
  1124.9 13.5 copy-start.17
  1124.9 13.5 copy-start.22
  1124.9 13.5 copy-start.25
Sparse Core Ops, SparseCore 0:
  10.9 158.4 all-gather.7
  172.3 75.6 all-gather.13
  250.4 54.5 all-gather.11
  307.3 54.4 all-gather.9
  364.5 144.6 all-gather.17
  511.9 142.7 all-gather.15
  657.5 142.7 all-gather.19
  803.8 69.0 reduce-scatter.4
  876.7 71.2 reduce-scatter.6
  1070.1 1667.5 reduce-scatter.8
  2740.6 494.9 reduce-scatter.10
where the time goes:
time: 3250 us; the launch traced here: 3240 us
  waiting for transfers between devices  2440 us (75%)
  matrix products  406 us (12%)
  local copies, waits for them, and re-layouts  152 us (5%)
  other arithmetic  142 us (4%)
  blocking collectives  90.1 us (3%)
    reduce_scatter x1, waiting for transfers between devices, body(): lax.psum_scatter(jnp.concatenate([inner(hidden_in, d_joint), inner(attend...  1530 us
    reduce_scatter x1, waiting for transfers between devices, body(): lax.psum_scatter(down_term, ('grp', 'tok'), scatter_dimension=0, tiled=True)  490 us
    all_gather x1, waiting for transfers between devices, body(): lax.all_gather(down_weight, ('grp', 'tok'), axis=0, tiled=True)  132 us
    all_gather x1, waiting for transfers between devices, body(): lax.all_gather(joint_weight, ('grp', 'tok'), axis=0, tiled=True)  111 us
    concatenate x1, other arithmetic, body(): jnp.concatenate([inner(hidden_in, d_joint), inner(attended_low, cotangent...  103 us
    dot_general x5, matrix products, inner(): lax.dot_general(left, right, (((0,), (0,)), ((), ())), preferred_element_...  90.1 us
    unnamed x2, blocking collectives  90.1 us
    reduce_scatter x1, waiting for transfers between devices, body(): lax.psum_scatter(d_values.reshape(-1, width).astype(jnp.bfloat16), 'tok',...  70.4 us
  transfers between devices with their start and end apart: 11, of which 8 were waited for; matrix products, arithmetic and copies ran while one was open for 18% of the time, Pallas kernels for 0%

commit v1 on v0

--- a/solution.py
+++ b/solution.py
@@ -13,6 +13,18 @@
 KEY_BLK = 256
 eps = 1e-05
 neg_big = -1e30
+
+
+def collect(shard, axis, dim):
+    ways, here = (lax.axis_size(axis), lax.axis_index(axis))
+    grown, reach = (shard, 1)
+    while reach < ways:
+        theirs = lax.ppermute(grown, axis, [(d, d ^ reach) for d in range(ways)])
+        mine_first = jnp.concatenate([grown, theirs], axis=dim)
+        theirs_first = jnp.concatenate([theirs, grown], axis=dim)
+        grown = jnp.where(here & reach == 0, mine_first, theirs_first)
+        reach = 2 * reach
+    return grown
 
 
 def spread_blocks(values):
@@ -76,7 +88,7 @@
     gathered = (
         lax.all_gather(norm_gain, ("grp", "tok"), axis=0, tiled=True),
         lax.all_gather(norm_bias, ("grp", "tok"), axis=0, tiled=True),
-        lax.all_gather(joint_weight, ("grp", "tok"), axis=0, tiled=True),
+        collect(joint_weight, ("grp", "tok"), 0),
         lax.all_gather(out_weight, ("grp", "tok"), axis=0, tiled=True),
         lax.all_gather(gate_weight, ("grp", "tok"), axis=0, tiled=True),
         lax.all_gather(up_weight, ("grp", "tok"), axis=0, tiled=True),

time: 3250 us -> 3930 us (1.21)
  blocking collectives: 90.1 us -> 614 us
  waiting for transfers between devices: 2440 us -> 2540 us
    unnamed x2, blocking collectives: 90.1 us -> 614 us
    ppermute x0 -> x5, waiting for transfers between devices: none -> 240 us  [collect(): theirs = lax.ppermute(grown, axis, [(d, d ^ reach) for d in range(ways)])]
    all_gather x1, waiting for transfers between devices: 111 us -> 0.01 us  [body(): lax.all_gather(joint_weight, ('grp', 'tok'), axis=0, tiled=True)]
    all_gather x1, waiting for transfers between devices: 47.7 us -> 0.01 us  [body(): lax.all_gather(out_weight, ('grp', 'tok'), axis=0, tiled=True)]
  transfers between devices with their start and end apart: 11 -> 16, of which waited for: 8 -> 10; matrix products, arithmetic and copies ran while one was open for 18% -> 18% of each run, Pallas kernels for 0% -> 0%
where the time goes in v1:
time: 3930 us; the launch traced here: 3920 us
  waiting for transfers between devices  2540 us (65%)
  blocking collectives  614 us (16%)
  matrix products  420 us (11%)
  other arithmetic  172 us (4%)
  local copies, waits for them, and re-layouts  151 us (4%)
    reduce_scatter x1, waiting for transfers between devices, body(): lax.psum_scatter(jnp.concatenate([inner(hidden_in, d_joint), inner(attend...  1570 us
    unnamed x2, blocking collectives  614 us
    reduce_scatter x1, waiting for transfers between devices, body(): lax.psum_scatter(down_term, ('grp', 'tok'), scatter_dimension=0, tiled=True)  490 us
    ppermute x5, waiting for transfers between devices, collect(): theirs = lax.ppermute(grown, axis, [(d, d ^ reach) for d in range(ways)])  240 us
    all_gather x1, waiting for transfers between devices, body(): lax.all_gather(down_weight, ('grp', 'tok'), axis=0, tiled=True)  121 us
    concatenate x1, other arithmetic, body(): jnp.concatenate([inner(hidden_in, d_joint), inner(attended_low, cotangent...  105 us
    dot_general x5, matrix products, inner(): lax.dot_general(left, right, (((0,), (0,)), ((), ())), preferred_element_...  92.6 us
  transfers between devices with their start and end apart: 16, of which 10 were waited for; matrix products, arithmetic and copies ran while one was open for 18% of the time, Pallas kernels for 0%

profile of v1, /device:TPU:1, one launch (start us, length us, event | category | flops | bytes accessed | tf_op | source)
XLA Modules:
  0.0 3919.2 jit_solution(5742176373894968393)
XLA Ops:
  13.9 34.6 collective-permute-done.1
  53.4 67.9 %collective-permute-done.2 = bf16[256,6144]{1,0:T(8,128)(2,1)} collective-permute-done((bf16[256,6144]{1,0:T(8,128)(2,1)}, bf16[256,6144]{1,0:T(8,128)(2,1)}, u32[]{:S(2)}, u32[]{:S(2)}) %collective-permute-start.2) | collective-permute-done | bytes 3145760 | tf_op jit(solution)/shard_map/ppermute | solution.py:22
  121.3 9.5 maximum_select_fusion.3
  131.8 134.6 %collective-permute-done.3 = bf16[512,6144]{1,0:T(8,128)(2,1)} collective-permute-done((bf16[512,6144]{1,0:T(8,128)(2,1)}, bf16[512,6144]{1,0:T(8,128)(2,1)}, u32[]{:S(2)}, u32[]{:S(2)}) %collective-permute-start.3) | collective-permute-done | bytes 6291488 | tf_op jit(solution)/shard_map/ppermute | solution.py:22
  266.4 15.9 maximum_select_fusion.2
  284.5 568.2 %all-reduce.5 = (bf16[2048]{0:T(1024)(128)(2,1)S(1)}, bf16[2048]{0:T(1024)(128)(2,1)S(1)}) all-reduce(bf16[2048]{0:T(1024)(128)(2,1)S(1)} %dynamic-update-slice.1, bf16[2048]{0:T(1024)(128)(2,1)S(1)} %dynamic-update-slice), channel_id=1, replica_groups=mesh['grp'=4,'tok'=8] {'grp','tok'}, use_global_device_ids=true, to_apply=%add.1 | all-reduce | flops 4096 | bytes 16384
  854.3 22.1 fusion.51
  896.1 7.4 convolution_convert_fusion
  907.8 38.2 all-gather.10.cloned.1.call-done
  946.1 10.6 copy.95
  956.6 9.0 copy.72
  965.6 41.3 %while.39 = (s32[]{:T(128)}, f32[32,256]{1,0:T(8,128)S(1)}, f32[32,256]{1,0:T(8,128)S(1)}, s32[256]{0:T(256)S(1)}, s32[8,256]{1,0:T(8,128)S(1)}, /*index=5*/s32[...) while((s32[]{:T(128)}, f32[32,256]{1,0:T(8,128)S(1)}, ...), condition=%wide.region_5.6_spmd.clone, body=%wide.region_2.5_spmd.clone.sunk | while | flops 285646848 | bytes 19510184 | solution.py:152
  1007.0 24.5 reshape.533
  1031.5 19.5 copy.71
  1051.1 52.7 %while.40 = (s32[]{:T(128)}, f32[256,32,64]{0,2,1:T(8,128)}, bf16[8,256,32,64]{1,3,2,0:T(8,128)(2,1)}, s32[256]{0:T(256)S(1)}, s32[8,256]{1,0:T(8,128)S(1)}, /*i...) while((s32[]{:T(128)}, f32[256,32,64]{0,2,1:T(8,128)}, ...), condition=%wide.region_7.8_spmd.clone, body=%wide.region_6.7_spmd.clone.sunk | while | flops 548798464 | bytes 7518634 | solution.py:169
  1051.5 5.7 bitcast_add_fusion.5
  1057.5 6.4 bitcast_add_fusion.5
  1064.1 6.4 bitcast_add_fusion.5
  1070.8 6.4 bitcast_add_fusion.5
  1077.4 6.4 bitcast_add_fusion.5
  1084.1 6.4 bitcast_add_fusion.5
  1090.7 6.4 bitcast_add_fusion.5
  1097.4 6.4 bitcast_add_fusion.5
  1106.0 121.6 %while.41 = (s32[]{:T(128)}, f32[256,32,64]{0,2,1:T(8,128)S(1)}, bf16[8,256,32,64]{1,3,2,0:T(8,128)(2,1)}, bf16[8,256,32,64]{1,3,2,0:T(8,128)(2,1)}, bf16[8,256,...) while((s32[]{:T(128)}, f32[256,32,64]{0,2,1:T(8,128)S(1)}, ...), condition=%wide.region_9.10_spmd.clone, body=%wide.region_8.9_spmd.clone.sunk | while | flops 1369833472 | bytes 57979896 | solution.py:227
  1227.6 15.4 copy.76
  1243.0 10.8 copy.96
  1253.8 15.3 copy.77
  1269.1 10.8 copy.97
  1283.7 9.9 fusion.97
  1293.6 13.3 fusion.89
  1306.9 13.4 fusion.91
  1320.3 121.0 %all-gather.18.cloned.1.call-done = bf16[5632,2048]{1,0:T(8,128)(2,1)} async-done(((bf16[176,2048]{1,0:T(8,128)(2,1)}), bf16[5632,2048]{1,0:T(8,128)(2,1)}) %all-gather.18.cloned.1.call-update) | async-done | bytes 23068688 | tf_op jit(solution)/shard_map/all_gather | solution.py:95
  1441.3 20.7 multiply_convert_fusion
  1462.0 21.5 fusion.84
  1483.4 20.8 fusion.86
  1504.3 9.6 reduce-scatter.5.cloned.1.call-done
  1517.0 71.9 %reduce-scatter.7.cloned.1.call-done = bf16[256,2048]{0,1:T(8,128)(2,1)} async-done(((bf16[2048,2048]{0,1:T(8,128)(2,1)}), bf16[256,2048]{0,1:T(8,128)(2,1)}) %reduce-scatter.7.cloned.1.call-update) | async-done | bytes 1048592 | tf_op jit(solution)/shard_map/reduce_scatter | solution.py:234
  1589.0 19.6 fusion.76
  1608.6 104.8 %pad_maximum_fusion = f32[2048,19456]{1,0:T(8,128)} fusion(f32[2048,5632]{1,0:T(8,128)} %fusion.84, f32[2048,5632]{1,0:T(8,128)} %fusion.86, f32[2048,2048]{1,0:T(8,128)} %fusion.97, f32[2048,6144]{1,0:T(8,128)} %fusion.76), kind=kLoop, calls=%fused_computation.67 | loop fusion | flops 119537664 | bytes 318767104 | tf_op jit(solution)/shard_map/concatenate | solution.py:257
  1714.6 20.9 fusion.98
  1737.0 6.3 convert_add_fusion
  1743.3 12.6 fusion.59
  1755.9 13.5 fusion.77
  1769.4 13.4 convolution_add_fusion.1
  1782.8 13.6 fusion.73
  1796.4 46.2 %all-reduce.4 = (f32[2048]{0:T(1024)S(1)}, f32[2048]{0:T(1024)S(1)}) all-reduce(f32[2048]{0:T(1024)S(1)} %get-tuple-element.483, f32[2048]{0:T(1024)S(1)} %get-tuple-element.486), channel_id=4, replica_groups=mesh['grp'=4,'tok'=8] {'grp','tok'}, use_global_device_ids=true, to_apply=%region_15.16.clone | all-reduce | flops 4096 | bytes 32768
  1847.2 1567.2 %reduce-scatter.9.cloned.1.call-done = f32[64,19456]{1,0:T(8,128)} async-done(((f32[2048,19456]{1,0:T(8,128)}), f32[64,19456]{1,0:T(8,128)}) %reduce-scatter.9.cloned.1.call-update) | async-done | bytes 4980752 | tf_op jit(solution)/shard_map/reduce_scatter | solution.py:256
  3422.6 489.9 %reduce-scatter.11.cloned.1.call-done = f32[176,2048]{1,0:T(8,128)} async-done(((f32[5632,2048]{1,0:T(8,128)}), f32[176,2048]{1,0:T(8,128)}) %reduce-scatter.11.cloned.1.call-update) | async-done | bytes 1441808 | tf_op jit(solution)/shard_map/reduce_scatter | solution.py:271
  (351 shorter events, 228.5 us)
Async XLA Ops:
  7.2 888.9 %all-gather.12.cloned.1.call-start = ((), (), s32[]{:S(2)}) async-start(), calls=%async_computation.6 | async-start | bytes 8650752 | tf_op jit(solution)/shard_map/all_gather | solution.py:92
  7.2 2.6 collective-permute-start
  11.5 37.0 collective-permute-start.1
  52.3 69.0 %collective-permute-start.2 = (bf16[256,6144]{1,0:T(8,128)(2,1)}, bf16[256,6144]{1,0:T(8,128)(2,1)}, u32[]{:S(2)}, u32[]{:S(2)}) collective-permute-start(bf16[256,6144]{1,0:T(8,128)(2,1)} %maximum_select_fusion.4), channel_id=1, source_target_pairs={{0,4},{1,5},{2,6},{3,7},{4,0},{5,1},{6,2},{7,3},{8,12},{9,13},{10,... | collective-permute-start | bytes 9437192 | tf_op jit(solution)/shard_map/ppermute | solution.py:22
  130.9 135.5 %collective-permute-start.3 = (bf16[512,6144]{1,0:T(8,128)(2,1)}, bf16[512,6144]{1,0:T(8,128)(2,1)}, u32[]{:S(2)}, u32[]{:S(2)}) collective-permute-start(bf16[512,6144]{1,0:T(8,128)(2,1)} %maximum_select_fusion.3), channel_id=1, source_target_pairs={{0,8},{1,9},{2,10},{3,11},{4,12},{5,13},{6,14},{7,15},{8,0},{9,1},... | collective-permute-start | bytes 18874376 | tf_op jit(solution)/shard_map/ppermute | solution.py:22
  131.8 152.2 %copy-start.28 = (bf16[64]{0:T(256)(128)(2,1)S(1)}, bf16[64]{0:T(256)(128)(2,1)}, u32[]{:S(2)}) copy-start(bf16[64]{0:T(256)(128)(2,1)} %param.19) | copy-start | bytes 388
  131.8 152.5 %copy-start.29 = (bf16[64]{0:T(256)(128)(2,1)S(1)}, bf16[64]{0:T(256)(128)(2,1)}, u32[]{:S(2)}) copy-start(bf16[64]{0:T(256)(128)(2,1)} %param.18) | copy-start | bytes 388
  131.8 720.9 %copy-start.27 = (s32[1,16]{1,0:T(1,128)S(1)}, s32[1,16]{1,0:T(1,128)}, u32[]{:S(2)}) copy-start(s32[1,16]{1,0:T(1,128)} %param.25) | copy-start | bytes 196
  131.8 721.1 %copy-start = (bf16[256,2048]{1,0:T(8,128)(2,1)S(1)}, bf16[256,2048]{1,0:T(8,128)(2,1)}, u32[]{:S(2)}) copy-start(bf16[256,2048]{1,0:T(8,128)(2,1)} %param.16) | copy-start | bytes 3145732
  282.3 572.0 %collective-permute-start.4 = (bf16[1024,6144]{1,0:T(8,128)(2,1)}, bf16[1024,6144]{1,0:T(8,128)(2,1)}, u32[]{:S(2)}, u32[]{:S(2)}) collective-permute-start(bf16[1024,6144]{1,0:T(8,128)(2,1)} %maximum_select_fusion.2), channel_id=1, source_target_pairs={{0,16},{1,17},{2,18},{3,19},{4,20},{5,21},{6,22},{7,23},{8,24},{9,... | collective-permute-start | bytes 37748744 | tf_op jit(solution)/shard_map/ppermute | solution.py:22
  283.9 662.2 %all-gather.10.cloned.1.call-start = ((), (), s32[]{:S(2)}) async-start(), calls=%async_computation.5 | async-start | bytes 9437184 | tf_op jit(solution)/shard_map/all_gather | solution.py:125
  852.6 1.6 copy-start.16
  853.1 23.3 copy-start.18
  853.5 22.8 copy-start.21
  854.3 32.7 copy-start.24
  888.3 7.8 copy-start.5
  889.4 117.6 %all-gather.8.cloned.1.call-start = ((), (), s32[]{:S(2)}) async-start(), calls=%async_computation.4 | async-start | bytes 9437184 | tf_op jit(solution)/shard_map/all_gather | solution.py:126
  892.2 401.3 %all-gather.16.cloned.1.call-start = ((), (), s32[]{:S(2)}) async-start(), calls=%async_computation.8 | async-start | bytes 23789568 | tf_op jit(solution)/shard_map/all_gather | solution.py:94
  892.8 414.1 %all-gather.14.cloned.1.call-start = ((), (), s32[]{:S(2)}) async-start(), calls=%async_computation.7 | async-start | bytes 23789568 | tf_op jit(solution)/shard_map/all_gather | solution.py:93
  893.4 547.9 %all-gather.18.cloned.1.call-start = ((), (), s32[]{:S(2)}) async-start(), calls=%async_computation.9 | async-start | bytes 23789568 | tf_op jit(solution)/shard_map/all_gather | solution.py:95
  893.9 619.9 %reduce-scatter.5.cloned.1.call-start = ((), (), s32[]{:S(2)}) async-start(), calls=%async_computation.10 | async-start | bytes 9437184 | tf_op jit(solution)/shard_map/reduce_scatter | solution.py:231
  1106.3 2.6 copy-start.8
  1121.4 2.6 copy-start.8
  1136.6 2.8 copy-start.8
  1152.0 2.6 copy-start.8
  1167.1 2.6 copy-start.8
  1182.3 2.6 copy-start.8
  1197.4 2.6 copy-start.8
  1212.5 2.6 copy-start.8
  1253.8 335.2 %reduce-scatter.7.cloned.1.call-start = ((), (), s32[]{:S(2)}) async-start(), calls=%async_computation.11 | async-start | bytes 9437184 | tf_op jit(solution)/shard_map/reduce_scatter | solution.py:234
  1279.9 475.9 %all-gather.20.cloned.1.call-start = ((), (), s32[]{:S(2)}) async-start(), calls=%async_computation.12 | async-start | bytes 25952256 | tf_op jit(solution)/shard_map/all_gather | solution.py:184
  1280.7 2133.8 %reduce-scatter.9.cloned.1.call-start = ((), (), s32[]{:S(2)}) async-start(), calls=%async_computation.13 | async-start | bytes 164364288 | tf_op jit(solution)/shard_map/reduce_scatter | solution.py:256
  1283.7 9.9 copy-start.1
  1283.7 9.9 copy-start.14
  1283.7 9.9 copy-start.17
  1283.7 9.9 copy-start.19
  1283.7 9.9 copy-start.22
  1504.3 12.3 copy-start.25
  1504.3 12.3 copy-start.26
  1513.8 2.9 copy-start.12
  1516.9 91.7 %copy-start.9 = (bf16[256,32,64]{0,2,1:T(8,128)(2,1)}, bf16[256,32,64]{0,2,1:T(8,128)(2,1)S(1)}, u32[]{:S(2)}) copy-start(bf16[256,32,64]{0,2,1:T(8,128)(2,1)S(1)} %pad_maximum_fusion.6) | copy-start | bytes 3145732
  1517.0 91.6 %copy-start.11 = (bf16[256,32,64]{0,2,1:T(8,128)(2,1)}, bf16[256,32,64]{0,2,1:T(8,128)(2,1)S(1)}, u32[]{:S(2)}) copy-start(bf16[256,32,64]{0,2,1:T(8,128)(2,1)S(1)} %pad_maximum_fusion.7) | copy-start | bytes 3145732
  1713.4 2199.1 %reduce-scatter.11.cloned.1.call-start = ((), (), s32[]{:S(2)}) async-start(), calls=%async_computation.14 | async-start | bytes 47579136 | tf_op jit(solution)/shard_map/reduce_scatter | solution.py:271
  1737.0 6.3 copy-start.7
  1743.3 12.6 copy-start.10
  1769.4 13.4 copy-start.15
  1769.4 13.4 copy-start.20
  1769.4 13.4 copy-start.23
  (5 other events, 6.8 us)
Sparse Core Ops, SparseCore 0:
  284.0 604.9 all-gather.11
  891.5 54.5 all-gather.9
  948.5 54.3 all-gather.7
  1005.6 144.6 all-gather.15
  1153.0 142.7 all-gather.13
  1298.5 142.7 all-gather.17
  1444.7 69.0 reduce-scatter.4
  1517.7 71.2 reduce-scatter.6
  1591.8 155.0 all-gather.19
  1749.2 1665.2 reduce-scatter.8
  3417.4 494.9 reduce-scatter.10
